TPU v7x, 32 devices: a whole 2x2x4 slice. The times are simulated.
32 devices in a mesh: tile: 4 (over y, core), dp: 8 (over z, x).
Axes of the slice: x: 2, y: 2, z: 4, core: 2. Of those that a mesh axis runs over, the one named last changes fastest.
Arguments:
- observed: float32 [8, 2, 8, 32], P('dp', None, 'tile'), may hold values from -6 to 6
- targets: float32 [8, 2, 8, 32], P('dp', None, 'tile'), may hold values from -6 to 6
- pixel_mask: int32 [8, 2, 8, 32], P('dp', None, 'tile'), may hold values 0 or 1
- lengths: int32 [8], P('dp'), may hold values from 1 to 2, as said below
- step_count: int32 [1], replicated, may hold values from 2 to 20
- kernels: float32 [1, 12800, 1024], P(None, 'dp'), may hold values from -0.0546875 to 0.0546875
- kernel_moment: float32 [1, 12800, 1024], P(None, 'dp'), may hold values from -7.6293945e-06 to 7.6293945e-06
- kernel_second: float32 [1, 12800, 1024], P(None, 'dp'), may hold values from 1.9073486e-12 to 7.6293945e-12
- norm_params: float32 [2, 1, 1024], replicated
- norm_moment: float32 [2, 1, 1024], replicated, may hold values from -1.5258789e-05 to 1.5258789e-05
- norm_second: float32 [2, 1, 1024], replicated, may hold values from 7.6293945e-12 to 3.0517578e-11
- end_params: float32 [3, 256], replicated
- end_moment: float32 [3, 256], replicated, may hold values from -7.6293945e-05 to 7.6293945e-05
- end_second: float32 [3, 256], replicated, may hold values from 1.9073486e-10 to 7.6293943e-10
- head_bias: float32 [1], replicated, may hold values from -3 to 3
- head_moment: float32 [1], replicated, may hold values from -0.0546875 to 0.0546875
- head_second: float32 [1], replicated, may hold values from 7.6293945e-05 to 0.00030517578
- hidden_init: float32 [1, 8, 8, 32, 256], P(None, 'dp', 'tile'), may hold values from -0.9 to 0.9
- cells_init: float32 [1, 8, 8, 32, 256], P(None, 'dp', 'tile'), may hold values from -5 to 5
Outputs:
- loss_value: float32 [], replicated
- grad_norm: float32 [], replicated
- kernels_new: float32 [1, 12800, 1024], P(None, 'dp')
- kernel_moment_new: float32 [1, 12800, 1024], P(None, 'dp')
- kernel_second_new: float32 [1, 12800, 1024], P(None, 'dp')
- norm_new: float32 [2, 1, 1024], replicated
- norm_moment_new: float32 [2, 1, 1024], replicated
- norm_second_new: float32 [2, 1, 1024], replicated
- end_new: float32 [3, 256], replicated
- end_moment_new: float32 [3, 256], replicated
- end_second_new: float32 [3, 256], replicated
- head_new: float32 [1], replicated
- head_moment_new: float32 [1], replicated
- head_second_new: float32 [1], replicated
- hidden_final: float32 [1, 8, 8, 32, 256], P(None, 'dp', 'tile')
- cells_final: float32 [1, 8, 8, 32, 256], P(None, 'dp', 'tile')
Inputs may be any that keep to these rules, and one draw needn't show every extreme that they name: `lengths`: some stream has all 2 frames counting and some only one.
All inputs are finite; a program needn't handle non-finite values. No bound on the sum of `pixel_mask` on one device may be relied on, other than what follows from the above.
Results may differ from a plain program's by a relative error of at most 0.0003.
The roundings to bfloat16 on the way count: a program that leaves them out, or rounds other values in their place, can miss the bound.
Values may be sent and summed in bfloat16 or wider, within the bound.
No kernel may reach another device: no remote copies, remote signals or barrier semaphores. Data moves between devices by JAX's collectives and lax.ppermute only.
A program may use at most 192 MiB of HBM per device.

v0:
```python
import jax
import jax.numpy as jnp
from jax import lax
from jax.sharding import PartitionSpec as P

IN_DIM = 512
KERNEL = 5
GROUP_SIZE = 64
clip_limit = 0.005
small_rate = 0.1


def padded_2(cells, sides, width):
    for axis, dim in sides:
        count = lax.axis_size(axis)
        ends = count - 1
        head = lax.slice_in_dim(cells, 0, width, axis=dim)
        tail = lax.slice_in_dim(cells, cells.shape[dim] - width, cells.shape[dim], axis=dim)
        cells = jnp.concatenate(
            [
                lax.ppermute(tail, axis, [(i, (i + 1) % count) for i in range(ends)]),
                cells,
                lax.ppermute(head, axis, [((i + 1) % count, i) for i in range(ends)]),
            ],
            axis=dim,
        )
    return cells


def group_norm(gates, gain, shift):
    full_shape = gates.shape
    grouped = gates.reshape(full_shape[:-1] + (full_shape[-1] // GROUP_SIZE, GROUP_SIZE))
    centred = grouped - jnp.mean(grouped, axis=-1, keepdims=True)
    spread = jnp.mean(centred * centred, axis=-1, keepdims=True)
    return (centred * lax.rsqrt(spread + 1e-05)).reshape(full_shape) * gain + shift


def lstm_cell(gates, cells_prev, gain, shift):
    normed = group_norm(gates, gain, shift)
    quarter = normed.shape[-1] // 4
    input_gate = jax.nn.sigmoid(normed[..., :quarter])
    forget_gate = jax.nn.sigmoid(normed[..., quarter : 2 * quarter])
    candidate = jnp.tanh(normed[..., 2 * quarter : 3 * quarter])
    output_gate = jax.nn.sigmoid(normed[..., 3 * quarter :])
    cells_next = forget_gate * cells_prev + input_gate * candidate
    return (output_gate * jnp.tanh(cells_next), cells_next)


def unfold(padded, rows, columns):
    pieces = []
    for row_off in range(KERNEL):
        for col_off in range(KERNEL):
            pieces.append(padded[:, row_off : row_off + rows, col_off : col_off + columns, :])
    joined = jnp.concatenate(pieces, axis=-1)
    return joined.reshape(-1, joined.shape[-1])


def pad_columns(values):
    margin = KERNEL // 2
    return jnp.pad(values, ((0, 0), (0, 0), (margin, margin), (0, 0)))


def layer_forward(weight_full, gain, shift, inputs_low, hidden_start, cells_start):
    rows, columns = (hidden_start.shape[1], hidden_start.shape[2])
    hidden_low = hidden_start.astype(jnp.bfloat16)
    cells = cells_start
    kept = []
    outputs = []
    outputs_low = []
    hidden = hidden_start
    for frame_no in range(len(inputs_low)):
        joined = jnp.concatenate([inputs_low[frame_no], hidden_low], axis=-1)
        padded = padded_2(joined, (("tile", 1),), KERNEL // 2)
        padded = pad_columns(padded)
        gates = jnp.dot(
            unfold(padded, rows, columns), weight_full, preferred_element_type=jnp.float32
        )
        gates = gates.reshape(hidden_start.shape[:3] + (weight_full.shape[1],))
        kept.append((padded, gates, cells))
        hidden, cells = lstm_cell(gates, cells, gain, shift)
        hidden_low = hidden.astype(jnp.bfloat16)
        outputs.append(hidden)
        outputs_low.append(hidden_low)
    return (outputs, outputs_low, kept, hidden, cells)


def layer_backward(weight_full, gain, shift, kept, grad_above):
    pixel_shape = kept[0][1].shape
    rows, columns, gate_dim = (pixel_shape[1], pixel_shape[2], pixel_shape[3])
    in_dim = weight_full.shape[0] // (KERNEL * KERNEL)
    half = in_dim // 2
    flipped = weight_full.reshape(KERNEL, KERNEL, in_dim, gate_dim)[::-1, ::-1]
    flipped = flipped.transpose(0, 1, 3, 2).reshape(KERNEL * KERNEL * gate_dim, in_dim)
    grad_weight = jnp.zeros(weight_full.shape, jnp.float32)
    grad_gain = jnp.zeros(gain.shape, jnp.float32)
    grad_shift = jnp.zeros(shift.shape, jnp.float32)
    grad_hidden = jnp.zeros(pixel_shape[:3] + (half,), jnp.float32)
    grad_cells = jnp.zeros(pixel_shape[:3] + (half,), jnp.float32)
    grad_inputs = [None] * len(kept)
    for frame_no in reversed(range(len(kept))):
        padded, gates, cells_prev = kept[frame_no]
        unused, pull = jax.vjp(lstm_cell, gates, cells_prev, gain, shift)
        grad_gates, grad_cells, part_gain, part_shift = pull(
            (grad_above[frame_no] + grad_hidden, grad_cells)
        )
        grad_gain = grad_gain + part_gain
        grad_shift = grad_shift + part_shift
        gates_low = grad_gates.astype(jnp.bfloat16)
        grad_weight = grad_weight + lax.dot_general(
            unfold(padded, rows, columns),
            gates_low.reshape(-1, gate_dim),
            (((0,), (0,)), ((), ())),
            preferred_element_type=jnp.float32,
        )
        spread = padded_2(gates_low, (("tile", 1),), KERNEL // 2)
        spread = pad_columns(spread)
        grad_joined = jnp.dot(
            unfold(spread, rows, columns), flipped, preferred_element_type=jnp.float32
        )
        grad_joined = grad_joined.reshape(pixel_shape[:3] + (in_dim,))
        grad_inputs[frame_no] = grad_joined[..., :half]
        grad_hidden = grad_joined[..., half:]
    return (grad_weight, grad_gain, grad_shift, grad_inputs)


def adamw(weight, moment, second, grad, rate, correction):
    moment_new = 0.5 * moment + 0.5 * grad
    second_new = 0.5 * second + 0.5 * grad * grad
    update = moment_new / correction / (jnp.sqrt(second_new / correction) + 1e-08)
    return (weight - rate * (update + 0.01 * weight), moment_new, second_new)


def per_device(
    observed,
    targets,
    pixel_mask,
    lengths,
    step_count,
    kernels,
    kernel_moment,
    kernel_second,
    norm_params,
    norm_moment,
    norm_second,
    end_params,
    end_moment,
    end_second,
    head_bias,
    head_moment,
    head_second,
    hidden_init,
    cells_init,
):
    frame_total = observed.shape[1]
    layers = kernels.shape[0]
    frame_ids = lax.broadcasted_iota(jnp.int32, (1, frame_total), 1)
    counted = (frame_ids < lengths[:, None]).astype(jnp.float32)
    valid = pixel_mask.astype(jnp.float32) * counted[:, :, None, None]
    count = jnp.maximum(lax.psum(jnp.sum(valid), ("tile", "dp")), 1.0)
    inputs_low = [
        (end_params[0] * observed[:, frame_no, :, :, None] + end_params[1]).astype(jnp.bfloat16)
        for frame_no in range(frame_total)
    ]
    outputs = []
    layer_no = 0
    weight_full = lax.all_gather(kernels[layer_no].astype(jnp.bfloat16), "dp", axis=0, tiled=True)
    outputs, outputs_low, kept, hidden, cells = layer_forward(
        weight_full,
        norm_params[0, layer_no],
        norm_params[1, layer_no],
        inputs_low,
        hidden_init[layer_no],
        cells_init[layer_no],
    )
    stored_kept = [kept]
    hidden_list = [hidden]
    cells_list = [cells]
    loss_sum = jnp.zeros((), jnp.float32)
    grad_head_weight = jnp.zeros(end_params.shape[1:], jnp.float32)
    grad_head = jnp.zeros((1,), jnp.float32)
    grad_above = []
    for frame_no in range(frame_total):
        predicted = jnp.sum(outputs[frame_no] * end_params[2], axis=-1) + head_bias[0]
        error = predicted - targets[:, frame_no]
        weighted = valid[:, frame_no] * error
        loss_sum = loss_sum + jnp.sum(weighted * error)
        grad_pred = 2.0 * weighted / count
        grad_head = grad_head + jnp.sum(grad_pred)
        grad_head_weight = grad_head_weight + jnp.sum(
            grad_pred[..., None] * outputs[frame_no], axis=(0, 1, 2)
        )
        grad_above.append(grad_pred[..., None] * end_params[2])
    kernel_grads = [None] * layers
    gain_grads = [None] * layers
    shift_grads = [None] * layers
    for layer_no in reversed(range(layers)):
        weight_full = lax.all_gather(
            kernels[layer_no].astype(jnp.bfloat16), "dp", axis=0, tiled=True
        )
        grad_weight, grad_gain, grad_shift, grad_inputs = layer_backward(
            weight_full,
            norm_params[0, layer_no],
            norm_params[1, layer_no],
            stored_kept[layer_no],
            grad_above,
        )
        kernel_grads[layer_no] = grad_weight
        gain_grads[layer_no] = grad_gain
        shift_grads[layer_no] = grad_shift
        grad_above = grad_inputs
    grad_lift_weight = jnp.zeros(end_params.shape[1:], jnp.float32)
    grad_lift_bias = jnp.zeros(end_params.shape[1:], jnp.float32)
    for frame_no in range(frame_total):
        grad_lift_weight = grad_lift_weight + jnp.sum(
            grad_above[frame_no] * observed[:, frame_no, :, :, None], axis=(0, 1, 2)
        )
        grad_lift_bias = grad_lift_bias + jnp.sum(grad_above[frame_no], axis=(0, 1, 2))
    grad_norms = jnp.stack([jnp.stack(gain_grads), jnp.stack(shift_grads)])
    grad_ends = jnp.stack([grad_lift_weight, grad_lift_bias, grad_head_weight])
    grad_kernels = jnp.stack(kernel_grads)
    shard = lax.psum_scatter(grad_kernels, "dp", scatter_dimension=1, tiled=True)
    shard = lax.psum(shard, "tile")
    local_square = jnp.sum(shard * shard)
    grad_norms, grad_ends, grad_head, loss_sum = lax.psum(
        (grad_norms, grad_ends, grad_head, loss_sum), ("tile", "dp")
    )
    kernel_square = lax.psum(local_square, "dp")
    squares = (
        kernel_square
        + jnp.sum(grad_norms * grad_norms)
        + jnp.sum(grad_ends * grad_ends)
        + jnp.sum(grad_head * grad_head)
    )
    grad_norm = jnp.sqrt(squares)
    factor = clip_limit / jnp.maximum(grad_norm, clip_limit)
    correction = 1.0 - jnp.power(0.5, step_count[0].astype(jnp.float32))
    kernel_rate = (KERNEL * KERNEL * IN_DIM) ** (-0.5)
    kern_out = adamw(kernels, kernel_moment, kernel_second, shard * factor, kernel_rate, correction)
    norm_out = adamw(
        norm_params, norm_moment, norm_second, grad_norms * factor, small_rate, correction
    )
    end_out = adamw(end_params, end_moment, end_second, grad_ends * factor, small_rate, correction)
    head_out = adamw(
        head_bias, head_moment, head_second, grad_head * factor, small_rate, correction
    )
    loss_value = loss_sum / count
    return (
        loss_value,
        grad_norm,
        kern_out[0],
        kern_out[1],
        kern_out[2],
        norm_out[0],
        norm_out[1],
        norm_out[2],
        end_out[0],
        end_out[1],
        end_out[2],
        head_out[0],
        head_out[1],
        head_out[2],
        jnp.stack(hidden_list),
        jnp.stack(cells_list),
    )


def solution(mesh):
    placed = (
        P("dp", None, "tile", None),
        P("dp", None, "tile", None),
        P("dp", None, "tile", None),
        P("dp"),
        P(),
        P(None, "dp", None),
        P(None, "dp", None),
        P(None, "dp", None),
        P(),
        P(),
        P(),
        P(),
        P(),
        P(),
        P(),
        P(),
        P(),
        P(None, "dp", "tile", None, None),
        P(None, "dp", "tile", None, None),
    )
    return jax.shard_map(
        per_device,
        mesh=mesh,
        in_specs=placed,
        out_specs=(
            P(),
            P(),
            P(None, "dp", None),
            P(None, "dp", None),
            P(None, "dp", None),
            P(),
            P(),
            P(),
            P(),
            P(),
            P(),
            P(),
            P(),
            P(),
            P(None, "dp", "tile", None, None),
            P(None, "dp", "tile", None, None),
        ),
        check_vma=False,
    )
```

profile of v0, /device:TPU:0, one launch (start us, length us, event | category | flops | bytes accessed | tf_op | source)
XLA Modules:
  0.0 1688.5 jit_solution(5633768059832277343)
XLA Ops:
  7.2 5.1 convert_element_type.95
  13.2 1.3 collective-permute-start.1
  14.5 3.0 collective-permute-start
  18.2 0.7 fusion.79
  18.9 85.6 %psum.50 = f32[]{:T(128)} all-reduce(f32[]{:T(128)} %get-tuple-element.65), channel_id=1, replica_groups=mesh['tile'=4,'dp'=8] {'tile','dp'}, use_global_device_ids=true, to_apply=%region_10.11 | all-reduce | flops 1 | bytes 8 | tf_op jit(solution)/shard_map/psum | solution.py:159
  107.0 1.2 copy-done.1
  108.5 408.1 %all-gather.3.cloned.1.call-done = bf16[1,12800,1024]{2,1,0:T(8,128)(2,1)} async-done(((bf16[1,1600,1024]{2,1,0:T(8,128)(2,1)}), bf16[1,12800,1024]{2,1,0:T(8,128)(2,1)}) %all-gather.3.cloned.1.call-update) | async-done | bytes 26214416 | tf_op jit(solution)/shard_map/all_gather | solution.py:166
  516.7 10.8 fusion.3
  529.2 0.8 multiply_add_fusion.2
  530.1 1.3 collective-permute-start.3
  531.4 3.0 collective-permute-start.2
  534.4 18.4 %reverse_bitcast_fusion = bf16[5,5,1024,512]{2,3,1,0:T(8,128)(2,1)} fusion(bf16[5,5,512,1024]{3,2,1,0:T(8,128)(2,1)} %bitcast.214), kind=kLoop, calls=%fused_computation.6 | loop fusion | bytes 52428800 | tf_op jit(solution)/shard_map/transpose | solution.py:93
  552.8 33.9 %copy.35 = bf16[5,5,1024,512]{3,2,1,0:T(8,128)(2,1)} copy(bf16[5,5,1024,512]{2,3,1,0:T(8,128)(2,1)} %reverse_bitcast_fusion) | data formatting | bytes 52428800 | tf_op jit(solution)/shard_map/transpose | solution.py:93
  588.0 0.7 copy-done
  588.8 10.8 fusion.1
  601.3 0.8 multiply_add_fusion.1
  602.0 0.7 fusion.74
  603.6 0.6 fusion.20
  605.0 1.0 fusion.25
  606.1 1.3 collective-permute-start.5
  607.4 3.8 collective-permute-start.4
  611.2 21.6 %fusion.11 = f32[12800,1024,1]{1,0,2:T(8,128)} fusion(bf16[1,2,32,12800]{3,2,1,0:T(8,128)(2,1)} %copy-done, bf16[1,2,32,1024]{3,2,1,0:T(8,128)(2,1)S(1)} %fusion.25), kind=kOutput, calls=%fused_computation.17 | convolution fusion | flops 1677721600 | bytes 54198272 | tf_op jit(solution)/shard_map/dot_general | solution.py:109
  633.8 10.8 fusion.13
  645.5 0.6 fusion.21
  646.9 1.0 fusion.27
  647.9 33.5 %fusion = f32[1,12800,1024]{2,1,0:T(8,128)} fusion(f32[12800,1024,1]{1,0,2:T(8,128)} %fusion.11, bf16[1,2,32,12800]{3,2,1,0:T(8,128)(2,1)S(1)} %copy-done.2, bf16[1,2,32,1024]{3,2,1,0:T(8,128)(2,1)S(1)} %fusion.27), kind=kOutput, calls=%fused_computation.1 | convolution fusion | flops 1690828800 | bytes 106627072 | tf_op jit(solution)/shard_map/dot_general | solution.py:109
  683.5 1.3 collective-permute-start.7
  684.8 4.5 collective-permute-start.6
  689.3 0.6 fusion.72
  692.8 0.7 constant_dynamic-update-slice_fusion.153
  693.4 0.7 constant_dynamic-update-slice_fusion.152
  694.1 0.7 constant_dynamic-update-slice_fusion.151
  694.8 0.7 constant_dynamic-update-slice_fusion.150
  695.5 0.7 constant_dynamic-update-slice_fusion.149
  696.2 0.7 constant_dynamic-update-slice_fusion.148
  696.8 0.7 constant_dynamic-update-slice_fusion.147
  697.5 0.7 constant_dynamic-update-slice_fusion.146
  698.2 0.7 constant_dynamic-update-slice_fusion.145
  698.9 0.7 constant_dynamic-update-slice_fusion.144
  699.6 0.7 constant_dynamic-update-slice_fusion.143
  700.2 0.7 constant_dynamic-update-slice_fusion.142
  700.9 0.7 constant_dynamic-update-slice_fusion.141
  701.6 0.7 constant_dynamic-update-slice_fusion.140
  702.3 0.7 constant_dynamic-update-slice_fusion.139
  703.0 0.7 constant_dynamic-update-slice_fusion.138
  703.6 0.7 constant_dynamic-update-slice_fusion.137
  704.3 0.7 constant_dynamic-update-slice_fusion.136
  705.0 0.7 constant_dynamic-update-slice_fusion.135
  705.7 793.9 %reduce-scatter.2.cloned.1.call-done = f32[1,1600,1024]{2,1,0:T(8,128)} async-done(((f32[1,12800,1024]{2,1,0:T(8,128)}), f32[1,1600,1024]{2,1,0:T(8,128)}) %reduce-scatter.2.cloned.1.call-update) | async-done | bytes 6553616 | tf_op jit(solution)/shard_map/reduce_scatter | solution.py:221
  1499.6 0.7 constant_dynamic-update-slice_fusion.134
  1500.3 0.7 constant_dynamic-update-slice_fusion.133
  1501.0 0.7 constant_dynamic-update-slice_fusion.132
  1501.7 0.7 constant_dynamic-update-slice_fusion.131
  1502.4 0.7 constant_dynamic-update-slice_fusion.130
  1503.0 0.7 constant_dynamic-update-slice_fusion.129
  1503.7 12.9 fusion.16
  1516.8 41.4 %all-reduce.12 = (f32[]{:T(128)}, f32[2,1,1024]{2,1,0:T(1,128)S(1)}, f32[3,256]{1,0:T(4,128)S(1)}, f32[1]{0:T(128)}) all-reduce(f32[]{:T(128)S(6)} %add.410, f32[2,1,1024]{2,1,0:T(1,128)S(1)} %pad_maximum_fusion.14, f32[3,256]{1,0:T(4,128)S(1)} %pad_maximum_fusion.15, f32[1]{0:T(128)} %bitcast.95), channel_id=1, replica_groups=mesh['tile'=4,'dp'=8] {'tile','dp'}, use_global_device_ids=true, to_apply=%region_8.9 | all-reduce | flops 2818 | bytes 22544 | tf_op jit(solution)/shard_map/psum | solution.py:224
  1559.4 0.6 multiply_reduce_fusion.13
  1560.1 66.4 %all-reduce.15.cloned.1.call-done = f32[1,1600,1024]{2,1,0:T(8,128)} async-done(((f32[1,1600,1024]{2,1,0:T(8,128)}), f32[1,1600,1024]{2,1,0:T(8,128)}) %all-reduce.15.cloned.1.call-update) | async-done | bytes 6553616 | tf_op jit(solution)/shard_map/psum | solution.py:222
  1626.4 5.1 multiply_reduce_fusion
  1632.9 22.0 %psum.52 = f32[]{:T(128)} all-reduce(f32[]{:T(128)} %multiply_reduce_fusion), channel_id=1, replica_groups=mesh['tile'=4,'dp'=8] {'dp'}, use_global_device_ids=true, to_apply=%region_18.19 | all-reduce | flops 1 | bytes 8 | tf_op jit(solution)/shard_map/psum | solution.py:227
  1657.7 0.7 multiply_subtract_fusion.1
  1658.4 0.6 multiply_subtract_fusion.2
  1659.0 17.3 %multiply_subtract_fusion = (f32[1,1600,1024]{2,1,0:T(8,128)}, f32[1,1600,1024]{2,1,0:T(8,128)}, f32[1,1600,1024]{2,1,0:T(8,128)}) fusion(f32[1,1600,1024]{2,1,0:T(8,128)} %param.24, f32[]{:T(128)} %bitcast.97, f32[1,1600,1024]{2,1,0:T(8,128)} %all-reduce.15.cloned.1.call-done, f32[]{:T(128)} %div.177, f32[1,1600,1024]{2,1,0:T(8,128)} %param.26, ...), kind=kLoop, calls=%fused_computation.10 | loop fusion | flops 24576000 | bytes 45875208 | tf_op jit(solution)/shard_map/sub | solution.py:130
  (249 shorter events, 11.2 us)
Async XLA Ops:
  7.2 509.5 %all-gather.3.cloned.1.call-start = ((), (), s32[]{:S(2)}) async-start(), calls=%async_computation.3 | async-start | bytes 29491200 | tf_op jit(solution)/shard_map/all_gather | solution.py:166
  12.3 0.7 copy-start.18
  12.3 0.7 copy-start.11
  12.3 0.9 copy-start.4
  12.3 5.9 copy-start.7
  12.3 5.9 copy-start.19
  12.4 1487.3 %reduce-scatter.2.cloned.1.call-start = ((), (), s32[]{:S(2)}) async-start(), calls=%async_computation.1 | async-start | bytes 58982400 | tf_op jit(solution)/shard_map/reduce_scatter | solution.py:221
  13.0 93.6 %copy-start.9 = (f32[2,32]{1,0:T(2,128)}, f32[2,32]{1,0:T(2,128)S(1)}, u32[]{:S(2)}) copy-start(f32[2,32]{1,0:T(2,128)S(1)} %get-tuple-element.135) | copy-start | bytes 772
  13.2 92.8 %collective-permute-start.1 = (bf16[1,2,32,512]{3,2,1,0:T(8,128)(2,1)S(1)}, bf16[1,2,32,512]{3,2,1,0:T(8,128)(2,1)S(1)}, u32[]{:S(2)}, u32[]{:S(2)}) collective-permute-start(bf16[1,2,32,512]{3,2,1,0:T(8,128)(2,1)S(1)} %pad_maximum_fusion.12), channel_id=1, source_target_pairs={{8,0},{16,8},{24,16},{9,1},{17,9},{25,17},{10,2},{18,10},{26,18},{... | collective-permute-start | bytes 196616 | tf_op jit(solution)/shard_map/ppermute | solution.py:23
  14.5 91.5 %collective-permute-start = (bf16[1,2,32,512]{3,2,1,0:T(8,128)(2,1)S(1)}, bf16[1,2,32,512]{3,2,1,0:T(8,128)(2,1)S(1)}, u32[]{:S(2)}, u32[]{:S(2)}) collective-permute-start(bf16[1,2,32,512]{3,2,1,0:T(8,128)(2,1)S(1)} %pad_maximum_fusion.12), channel_id=1, source_target_pairs={{0,8},{8,16},{16,24},{1,9},{9,17},{17,25},{2,10},{10,18},{18,26},{... | collective-permute-start | bytes 196616 | tf_op jit(solution)/shard_map/ppermute | solution.py:21
  107.0 1.2 copy-start.1
  528.8 1.2 copy-start.5
  530.1 56.6 %collective-permute-start.3 = (bf16[1,2,32,512]{3,2,1,0:T(8,128)(2,1)S(1)}, bf16[1,2,32,512]{3,2,1,0:T(8,128)(2,1)S(1)}, u32[]{:S(2)}, u32[]{:S(2)}) collective-permute-start(bf16[1,2,32,512]{3,2,1,0:T(8,128)(2,1)S(1)} %pad_maximum_fusion.13), channel_id=1, source_target_pairs={{8,0},{16,8},{24,16},{9,1},{17,9},{25,17},{10,2},{18,10},{26,18},{... | collective-permute-start | bytes 196616 | tf_op jit(solution)/shard_map/ppermute | solution.py:23
  531.4 55.3 %collective-permute-start.2 = (bf16[1,2,32,512]{3,2,1,0:T(8,128)(2,1)S(1)}, bf16[1,2,32,512]{3,2,1,0:T(8,128)(2,1)S(1)}, u32[]{:S(2)}, u32[]{:S(2)}) collective-permute-start(bf16[1,2,32,512]{3,2,1,0:T(8,128)(2,1)S(1)} %pad_maximum_fusion.13), channel_id=1, source_target_pairs={{0,8},{8,16},{16,24},{1,9},{9,17},{17,25},{2,10},{10,18},{18,26},{... | collective-permute-start | bytes 196616 | tf_op jit(solution)/shard_map/ppermute | solution.py:21
  587.6 1.2 copy-start
  601.1 1.8 copy-start.15
  602.8 41.9 %copy-start.3 = (f32[1,2,32,256]{3,2,1,0:T(8,128)}, f32[1,2,32,256]{3,2,1,0:T(8,128)S(1)}, u32[]{:S(2)}) copy-start(f32[1,2,32,256]{3,2,1,0:T(8,128)S(1)} %get-tuple-element.37) | copy-start | bytes 196612
  606.1 26.7 %collective-permute-start.5 = (bf16[1,2,32,1024]{3,2,1,0:T(8,128)(2,1)S(1)}, bf16[1,2,32,1024]{3,2,1,0:T(8,128)(2,1)S(1)}, u32[]{:S(2)}, u32[]{:S(2)}) collective-permute-start(bf16[1,2,32,1024]{3,2,1,0:T(8,128)(2,1)S(1)} %fusion.25), channel_id=1, source_target_pairs={{8,0},{16,8},{24,16},{9,1},{17,9},{25,17},{10,2},{18,10},{26,18},{... | collective-permute-start | bytes 393224 | tf_op jit(solution)/shard_map/ppermute | solution.py:23
  607.4 25.4 %collective-permute-start.4 = (bf16[1,2,32,1024]{3,2,1,0:T(8,128)(2,1)S(1)}, bf16[1,2,32,1024]{3,2,1,0:T(8,128)(2,1)S(1)}, u32[]{:S(2)}, u32[]{:S(2)}) collective-permute-start(bf16[1,2,32,1024]{3,2,1,0:T(8,128)(2,1)S(1)} %fusion.25), channel_id=1, source_target_pairs={{0,8},{8,16},{16,24},{1,9},{9,17},{17,25},{2,10},{10,18},{18,26},{... | collective-permute-start | bytes 393224 | tf_op jit(solution)/shard_map/ppermute | solution.py:21
  633.8 11.0 copy-start.6
  646.3 1.6 copy-start.2
  681.5 944.9 %all-reduce.15.cloned.1.call-start = ((), (), s32[]{:S(2)}) async-start(), calls=%async_computation.2 | async-start | bytes 13107200 | tf_op jit(solution)/shard_map/psum | solution.py:222
  683.5 9.1 collective-permute-start.7
  684.8 7.8 collective-permute-start.6
  1503.7 12.9 copy-start.10
  1560.0 97.7 %copy-start.8 = (f32[2,1,1024]{2,1,0:T(1,128)S(1)}, f32[2,1,1024]{2,1,0:T(1,128)}, u32[]{:S(2)}) copy-start(f32[2,1,1024]{2,1,0:T(1,128)} %param.27) | copy-start | bytes 24580
  1560.0 97.7 %copy-start.13 = (f32[2,1,1024]{2,1,0:T(1,128)S(1)}, f32[2,1,1024]{2,1,0:T(1,128)}, u32[]{:S(2)}) copy-start(f32[2,1,1024]{2,1,0:T(1,128)} %param.29) | copy-start | bytes 24580
  1560.0 97.7 %copy-start.14 = (f32[2,1,1024]{2,1,0:T(1,128)S(1)}, f32[2,1,1024]{2,1,0:T(1,128)}, u32[]{:S(2)}) copy-start(f32[2,1,1024]{2,1,0:T(1,128)} %param.28) | copy-start | bytes 24580
  1560.0 98.3 %copy-start.12 = (f32[3,256]{1,0:T(4,128)S(1)}, f32[3,256]{1,0:T(4,128)}, u32[]{:S(2)}) copy-start(f32[3,256]{1,0:T(4,128)} %param.30) | copy-start | bytes 9220
  1560.0 98.3 %copy-start.16 = (f32[3,256]{1,0:T(4,128)S(1)}, f32[3,256]{1,0:T(4,128)}, u32[]{:S(2)}) copy-start(f32[3,256]{1,0:T(4,128)} %param.32) | copy-start | bytes 9220
  1560.0 98.3 %copy-start.17 = (f32[3,256]{1,0:T(4,128)S(1)}, f32[3,256]{1,0:T(4,128)}, u32[]{:S(2)}) copy-start(f32[3,256]{1,0:T(4,128)} %param.31) | copy-start | bytes 9220
Sparse Core Ops, SparseCore 0:
  12.5 504.1 all-gather.2
  681.6 817.9 reduce-scatter.1
  1502.0 124.3 all-reduce.14
where the time goes:
time: 1690 us
  waiting for transfers between devices  1270 us (75%)
  blocking collectives  149 us (9%)
  matrix products  100 us (6%)
  local copies, waits for them, and re-layouts  76.5 us (5%)
  other arithmetic  41.9 us (2%)
  between operations  32.4 us (2%)
  starting transfers between devices  19.7 us (1%)
    reduce_scatter x1, waiting for transfers between devices, per_device(): lax.psum_scatter(grad_kernels, 'dp', scatter_dimension=1, tiled=True)  794 us
    all_gather x1, waiting for transfers between devices, per_device(): lax.all_gather(kernels[layer_no].astype(jnp.bfloat16), 'dp', axis=0, tile...  408 us
    psum x1, blocking collectives, per_device(): count = jnp.maximum(lax.psum(jnp.sum(valid), ('tile', 'dp')), 1.0)  85.6 us
    psum x1, waiting for transfers between devices, per_device(): shard = lax.psum(shard, 'tile')  66.4 us
    dot_general x2, matrix products, layer_backward(): lax.dot_general(unfold(padded, rows, columns), gates_low.reshape(-1, gate...  55.1 us
    transpose x2, local copies, waits for them, and re-layouts, layer_backward(): flipped.transpose(0, 1, 3, 2).reshape(KERNEL * KERNEL * gate_dim, in_dim)  52.3 us
    psum x1, blocking collectives, per_device(): lax.psum((grad_norms, grad_ends, grad_head, loss_sum), ('tile', 'dp'))  41.4 us
  transfers between devices with their start and end apart: 11, of which 3 were waited for; matrix products, arithmetic and copies ran while one was open for 6% of the time, Pallas kernels for 0%

commit v1 on v0

--- a/solution.py
+++ b/solution.py
@@ -8,6 +8,24 @@
 GROUP_SIZE = 64
 clip_limit = 0.005
 small_rate = 0.1
+
+
+def gather_around(value, axis, dim):
+    ways, here, turn = (lax.axis_size(axis), lax.axis_index(axis), value.shape[dim])
+    shape = [n * ways if d == dim else n for d, n in enumerate(value.shape)]
+    full = lax.dynamic_update_slice_in_dim(
+        jnp.zeros(shape, value.dtype), value, here * turn, axis=dim
+    )
+    going_up = going_down = value
+    for far in range(1, ways // 2 + 1):
+        going_up = lax.ppermute(going_up, axis, [(d, (d + 1) % ways) for d in range(ways)])
+        full = lax.dynamic_update_slice_in_dim(full, going_up, (here - far) % ways * turn, axis=dim)
+        if 2 * far < ways:
+            going_down = lax.ppermute(going_down, axis, [(d, (d - 1) % ways) for d in range(ways)])
+            full = lax.dynamic_update_slice_in_dim(
+                full, going_down, (here + far) % ways * turn, axis=dim
+            )
+    return full
 
 
 def padded_2(cells, sides, width):
@@ -163,7 +181,7 @@
     ]
     outputs = []
     layer_no = 0
-    weight_full = lax.all_gather(kernels[layer_no].astype(jnp.bfloat16), "dp", axis=0, tiled=True)
+    weight_full = gather_around(kernels[layer_no].astype(jnp.bfloat16), "dp", 0)
     outputs, outputs_low, kept, hidden, cells = layer_forward(
         weight_full,
         norm_params[0, layer_no],

time: 1690 us -> 2260 us (1.34)
  waiting for transfers between devices: 1270 us -> 1810 us
  local copies, waits for them, and re-layouts: 76.5 us -> 122 us
  blocking collectives: 149 us -> 104 us
    ppermute x0 -> x7, waiting for transfers between devices: none -> 949 us  [the longest x4 563 us: gather_around(): lax.ppermute(going_up, axis, [(d, (d + 1) % ways) for d in range(ways)])]
    all_gather x1, waiting for transfers between devices: 408 us -> 0.01 us  [per_device(): lax.all_gather(kernels[layer_no].astype(jnp.bfloat16), 'dp', axis=0, tile...]
    psum x1, blocking collectives: 85.6 us -> 40.8 us  [per_device(): count = jnp.maximum(lax.psum(jnp.sum(valid), ('tile', 'dp')), 1.0)]
  transfers between devices with their start and end apart: 11 -> 18, of which waited for: 3 -> 7; matrix products, arithmetic and copies ran while one was open for 6% -> 6% of each run, Pallas kernels for 0% -> 0%
where the time goes in v1:
time: 2260 us
  waiting for transfers between devices  1810 us (80%)
  local copies, waits for them, and re-layouts  122 us (5%)
  blocking collectives  104 us (5%)
  matrix products  101 us (4%)
  other arithmetic  45 us (2%)
  starting transfers between devices  41.6 us (2%)
  between operations  32.3 us (1%)
    reduce_scatter x1, waiting for transfers between devices, per_device(): lax.psum_scatter(grad_kernels, 'dp', scatter_dimension=1, tiled=True)  793 us
    ppermute x4, waiting for transfers between devices, gather_around(): lax.ppermute(going_up, axis, [(d, (d + 1) % ways) for d in range(ways)])  563 us
    ppermute x3, waiting for transfers between devices, gather_around(): lax.ppermute(going_down, axis, [(d, (d - 1) % ways) for d in range(ways)])  386 us
    psum x1, waiting for transfers between devices, per_device(): shard = lax.psum(shard, 'tile')  66.4 us
    dot_general x2, matrix products, layer_backward(): lax.dot_general(unfold(padded, rows, columns), gates_low.reshape(-1, gate...  55.1 us
    transpose x2, local copies, waits for them, and re-layouts, layer_backward(): flipped.transpose(0, 1, 3, 2).reshape(KERNEL * KERNEL * gate_dim, in_dim)  52.1 us
  transfers between devices with their start and end apart: 18, of which 7 were waited for; matrix products, arithmetic and copies ran while one was open for 6% of the time, Pallas kernels for 0%

profile of v1, /device:TPU:0, one launch (start us, length us, event | category | flops | bytes accessed | tf_op | source)
XLA Modules:
  0.0 2255.1 jit_solution(9720250116042049880)
XLA Ops:
  7.2 10.3 broadcast_in_dim.22
  17.5 3.7 constant_dynamic-update-slice_fusion.161
  21.3 1.8 copy-done.1
  23.2 3.0 collective-permute-start.2
  28.1 1.3 collective-permute-start.1
  29.3 3.0 collective-permute-start
  32.4 3.1 collective-permute-start.3
  35.5 0.8 convert_element_type.91
  37.6 0.7 fusion.76
  39.0 291.7 %collective-permute-done.2 = bf16[1600,1024]{1,0:T(8,128)(2,1)} collective-permute-done((bf16[1600,1024]{1,0:T(8,128)(2,1)S(1)}, bf16[1600,1024]{1,0:T(8,128)(2,1)}, u32[]{:S(2)}, u32[]{:S(2)}) %collective-permute-start.2) | collective-permute-done | bytes 3276832 | tf_op jit(solution)/shard_map/ppermute | solution.py:21
  330.7 2.6 collective-permute-start.4
  333.7 117.9 %collective-permute-done.3 = bf16[1600,1024]{1,0:T(8,128)(2,1)} collective-permute-done((bf16[1600,1024]{1,0:T(8,128)(2,1)S(1)}, bf16[1600,1024]{1,0:T(8,128)(2,1)}, u32[]{:S(2)}, u32[]{:S(2)}) %collective-permute-start.3) | collective-permute-done | bytes 3276832 | tf_op jit(solution)/shard_map/ppermute | solution.py:24
  452.2 1.5 collective-permute-start.6
  454.2 268.6 %collective-permute-done.5 = bf16[1600,1024]{1,0:T(8,128)(2,1)S(1)} collective-permute-done((bf16[1600,1024]{1,0:T(8,128)(2,1)}, bf16[1600,1024]{1,0:T(8,128)(2,1)S(1)}, u32[]{:S(2)}, u32[]{:S(2)}) %collective-permute-start.5) | collective-permute-done | bytes 3276832 | tf_op jit(solution)/shard_map/ppermute | solution.py:24
  722.9 140.6 %collective-permute-done.6 = bf16[1600,1024]{1,0:T(8,128)(2,1)S(1)} collective-permute-done((bf16[1600,1024]{1,0:T(8,128)(2,1)S(1)}, bf16[1600,1024]{1,0:T(8,128)(2,1)S(1)}, u32[]{:S(2)}, u32[]{:S(2)}) %collective-permute-start.6) | collective-permute-done | bytes 3276832 | tf_op jit(solution)/shard_map/ppermute | solution.py:21
  863.6 11.3 collective-permute-start.8
  875.0 4.0 constant_dynamic-update-slice_fusion.160
  879.0 4.0 constant_dynamic-update-slice_fusion.159
  883.0 2.1 constant_dynamic-update-slice_fusion.158
  885.1 2.1 constant_dynamic-update-slice_fusion.157
  887.1 2.0 constant_dynamic-update-slice_fusion.156
  889.2 2.0 constant_dynamic-update-slice_fusion.155
  891.2 130.3 %collective-permute-done.8 = bf16[1600,1024]{1,0:T(8,128)(2,1)S(1)} collective-permute-done((bf16[1600,1024]{1,0:T(8,128)(2,1)S(1)}, bf16[1600,1024]{1,0:T(8,128)(2,1)S(1)}, u32[]{:S(2)}, u32[]{:S(2)}) %collective-permute-start.8) | collective-permute-done | bytes 3276832 | tf_op jit(solution)/shard_map/ppermute | solution.py:21
  1021.5 2.0 constant_dynamic-update-slice_fusion.154
  1023.5 10.8 fusion.79
  1036.0 0.8 multiply_add_fusion.2
  1036.9 1.3 collective-permute-start.10
  1038.2 3.0 collective-permute-start.9
  1041.9 40.8 %psum.50 = f32[]{:T(128)} all-reduce(f32[]{:T(128)} %get-tuple-element.67), channel_id=1, replica_groups=mesh['tile'=4,'dp'=8] {'tile','dp'}, use_global_device_ids=true, to_apply=%region_10.11 | all-reduce | flops 1 | bytes 8 | tf_op jit(solution)/shard_map/psum | solution.py:177
  1085.5 0.8 copy-done.2
  1086.3 10.8 fusion.80
  1098.8 0.8 multiply_add_fusion.1
  1099.6 0.7 fusion.70
  1103.1 1.0 fusion.21
  1104.1 1.3 collective-permute-start.12
  1105.4 3.3 collective-permute-start.11
  1108.7 21.6 fusion.7
  1131.1 0.7 constant_dynamic-update-slice_fusion.127
  1132.5 0.7 constant_dynamic-update-slice_fusion.125
  1133.2 0.7 constant_dynamic-update-slice_fusion.124
  1134.5 0.7 constant_dynamic-update-slice_fusion.122
  1135.9 0.7 constant_dynamic-update-slice_fusion.120
  1136.6 0.7 constant_dynamic-update-slice_fusion.119
  1139.3 0.7 constant_dynamic-update-slice_fusion.115
  1140.0 0.7 constant_dynamic-update-slice_fusion.114
  1142.7 0.7 constant_dynamic-update-slice_fusion.110
  1143.4 0.7 constant_dynamic-update-slice_fusion.109
  1146.1 0.7 constant_dynamic-update-slice_fusion.105
  1147.4 18.2 reverse_bitcast_fusion
  1165.6 33.9 %copy.35 = bf16[5,5,1024,512]{3,2,1,0:T(8,128)(2,1)} copy(bf16[5,5,1024,512]{2,3,1,0:T(8,128)(2,1)} %reverse_bitcast_fusion) | data formatting | bytes 52428800 | tf_op jit(solution)/shard_map/transpose | solution.py:111
  1199.5 11.7 fusion.9
  1211.2 0.7 multiply_reduce_fusion.9
  1214.0 1.0 fusion.23
  1215.1 33.5 %fusion = f32[1,12800,1024]{2,1,0:T(8,128)} fusion(f32[12800,1024,1]{1,0,2:T(8,128)} %fusion.7, bf16[1,2,32,12800]{3,2,1,0:T(8,128)(2,1)S(1)} %copy-done.4, bf16[1,2,32,1024]{3,2,1,0:T(8,128)(2,1)S(1)} %fusion.23), kind=kOutput, calls=%fused_computation.1 | convolution fusion | flops 1690828800 | bytes 106627072 | tf_op jit(solution)/shard_map/dot_general | solution.py:127
  1250.7 1.3 collective-permute-start.14
  1252.0 4.9 collective-permute-start.13
  1273.2 793.1 %reduce-scatter.2.cloned.1.call-done = f32[1,1600,1024]{2,1,0:T(8,128)} async-done(((f32[1,12800,1024]{2,1,0:T(8,128)}), f32[1,1600,1024]{2,1,0:T(8,128)}) %reduce-scatter.2.cloned.1.call-update) | async-done | bytes 6553616 | tf_op jit(solution)/shard_map/reduce_scatter | solution.py:239
  2066.3 0.7 constant_dynamic-update-slice_fusion.134
  2070.4 12.9 fusion.12
  2083.4 41.3 %all-reduce.12 = (f32[]{:T(128)}, f32[2,1,1024]{2,1,0:T(1,128)S(1)}, f32[3,256]{1,0:T(4,128)S(1)}, f32[1]{0:T(128)}) all-reduce(f32[]{:T(128)S(6)} %add.487, f32[2,1,1024]{2,1,0:T(1,128)S(1)} %pad_maximum_fusion.14, f32[3,256]{1,0:T(4,128)S(1)} %pad_maximum_fusion.15, f32[1]{0:T(128)} %bitcast.95), channel_id=1, replica_groups=mesh['tile'=4,'dp'=8] {'tile','dp'}, use_global_device_ids=true, to_apply=%region_8.9 | all-reduce | flops 2818 | bytes 22544 | tf_op jit(solution)/shard_map/psum | solution.py:242
  2126.7 66.4 %all-reduce.15.cloned.1.call-done = f32[1,1600,1024]{2,1,0:T(8,128)} async-done(((f32[1,1600,1024]{2,1,0:T(8,128)}), f32[1,1600,1024]{2,1,0:T(8,128)}) %all-reduce.15.cloned.1.call-update) | async-done | bytes 6553616 | tf_op jit(solution)/shard_map/psum | solution.py:240
  2193.1 5.1 multiply_reduce_fusion
  2199.6 22.0 psum.52
  2225.7 17.3 multiply_subtract_fusion
  (295 shorter events, 43.8 us)
Async XLA Ops:
  7.2 1140.3 %all-gather.3.cloned.1.call-start = ((), (), s32[]{:S(2)}) async-start(), calls=%async_computation.3 | async-start | bytes 29491200 | tf_op jit(solution)/shard_map/all_gather | solution.py:215
  7.2 10.3 copy-start
  17.5 8.6 copy-start.27
  17.5 9.2 copy-start.17
  21.2 1.9 copy-start.1
  21.2 6.2 copy-start.6
  21.3 2045.0 %reduce-scatter.2.cloned.1.call-start = ((), (), s32[]{:S(2)}) async-start(), calls=%async_computation.1 | async-start | bytes 58982400 | tf_op jit(solution)/shard_map/reduce_scatter | solution.py:239
  23.2 307.5 %collective-permute-start.2 = (bf16[1600,1024]{1,0:T(8,128)(2,1)S(1)}, bf16[1600,1024]{1,0:T(8,128)(2,1)}, u32[]{:S(2)}, u32[]{:S(2)}) collective-permute-start(bf16[1600,1024]{1,0:T(8,128)(2,1)S(1)} %bitcast.216), channel_id=1, source_target_pairs={{0,1},{1,2},{2,3},{3,4},{4,5},{5,6},{6,7},{7,0},{8,9},{9,10},{10,1... | collective-permute-start | bytes 9830408 | tf_op jit(solution)/shard_map/ppermute | solution.py:21
  26.7 5.7 copy-start.12
  26.7 5.7 copy-start.15
  28.1 10.8 collective-permute-start.1
  29.3 9.5 collective-permute-start
  32.4 419.2 %collective-permute-start.3 = (bf16[1600,1024]{1,0:T(8,128)(2,1)S(1)}, bf16[1600,1024]{1,0:T(8,128)(2,1)}, u32[]{:S(2)}, u32[]{:S(2)}) collective-permute-start(bf16[1600,1024]{1,0:T(8,128)(2,1)S(1)} %bitcast.217), channel_id=1, source_target_pairs={{0,7},{1,0},{2,1},{3,2},{4,3},{5,4},{6,5},{7,6},{8,15},{9,8},{10,9... | collective-permute-start | bytes 9830408 | tf_op jit(solution)/shard_map/ppermute | solution.py:24
  37.6 295.9 %copy-start.13 = (f32[2,32]{1,0:T(2,128)S(1)}, f32[2,32]{1,0:T(2,128)}, u32[]{:S(2)}) copy-start(f32[2,32]{1,0:T(2,128)} %copy-done.12) | copy-start | bytes 772
  37.6 296.0 %copy-start.7 = (f32[1,1,2,32,256]{4,3,2,1,0:T(8,128)S(1)}, f32[1,1,2,32,256]{4,3,2,1,0:T(8,128)}, u32[]{:S(2)}) copy-start(f32[1,1,2,32,256]{4,3,2,1,0:T(8,128)} %param.36) | copy-start | bytes 196612
  330.7 121.5 %collective-permute-start.4 = (bf16[1600,1024]{1,0:T(8,128)(2,1)}, bf16[1600,1024]{1,0:T(8,128)(2,1)S(1)}, u32[]{:S(2)}, u32[]{:S(2)}) collective-permute-start(bf16[1600,1024]{1,0:T(8,128)(2,1)} %collective-permute-done.2), channel_id=1, source_target_pairs={{0,1},{1,2},{2,3},{3,4},{4,5},{5,6},{6,7},{7,0},{8,9},{9,10},{10,1... | collective-permute-start | bytes 9830408 | tf_op jit(solution)/shard_map/ppermute | solution.py:21
  451.6 271.2 %collective-permute-start.5 = (bf16[1600,1024]{1,0:T(8,128)(2,1)}, bf16[1600,1024]{1,0:T(8,128)(2,1)S(1)}, u32[]{:S(2)}, u32[]{:S(2)}) collective-permute-start(bf16[1600,1024]{1,0:T(8,128)(2,1)} %collective-permute-done.3), channel_id=1, source_target_pairs={{0,7},{1,0},{2,1},{3,2},{4,3},{5,4},{6,5},{7,6},{8,15},{9,8},{10,9... | collective-permute-start | bytes 9830408 | tf_op jit(solution)/shard_map/ppermute | solution.py:24
  452.2 411.4 %collective-permute-start.6 = (bf16[1600,1024]{1,0:T(8,128)(2,1)S(1)}, bf16[1600,1024]{1,0:T(8,128)(2,1)S(1)}, u32[]{:S(2)}, u32[]{:S(2)}) collective-permute-start(bf16[1600,1024]{1,0:T(8,128)(2,1)S(1)} %collective-permute-done.4), channel_id=1, source_target_pairs={{0,1},{1,2},{2,3},{3,4},{4,5},{5,6},{6,7},{7,0},{8,9},{9,10},{10,1... | collective-permute-start | bytes 9830408 | tf_op jit(solution)/shard_map/ppermute | solution.py:21
  453.9 268.9 %copy-start.30 = (f32[64]{0:T(128)S(1)}, f32[64]{0:T(128)}, u32[]{:S(2)}) copy-start(f32[64]{0:T(128)} %mul.817) | copy-start | bytes 772
  454.1 409.5 %copy-start.3 = (bf16[1,2,32,12800]{3,2,1,0:T(8,128)(2,1)}, bf16[1,2,32,12800]{3,2,1,0:T(8,128)(2,1)S(1)}, u32[]{:S(2)}) copy-start(bf16[1,2,32,12800]{3,2,1,0:T(8,128)(2,1)S(1)} %get-tuple-element.80) | copy-start | bytes 4915204
  722.8 166.4 %collective-permute-start.7 = (bf16[1600,1024]{1,0:T(8,128)(2,1)S(1)}, bf16[1600,1024]{1,0:T(8,128)(2,1)S(1)}, u32[]{:S(2)}, u32[]{:S(2)}) collective-permute-start(bf16[1600,1024]{1,0:T(8,128)(2,1)S(1)} %collective-permute-done.5), channel_id=1, source_target_pairs={{0,7},{1,0},{2,1},{3,2},{4,3},{5,4},{6,5},{7,6},{8,15},{9,8},{10,9... | collective-permute-start | bytes 9830408 | tf_op jit(solution)/shard_map/ppermute | solution.py:24
  863.6 157.9 %collective-permute-start.8 = (bf16[1600,1024]{1,0:T(8,128)(2,1)S(1)}, bf16[1600,1024]{1,0:T(8,128)(2,1)S(1)}, u32[]{:S(2)}, u32[]{:S(2)}) collective-permute-start(bf16[1600,1024]{1,0:T(8,128)(2,1)S(1)} %collective-permute-done.6), channel_id=1, source_target_pairs={{0,1},{1,2},{2,3},{3,4},{4,5},{5,6},{6,7},{7,0},{8,9},{9,10},{10,1... | collective-permute-start | bytes 9830408 | tf_op jit(solution)/shard_map/ppermute | solution.py:21
  1035.6 1.2 copy-start.8
  1035.6 5.6 copy-start.28
  1035.6 5.6 copy-start.31
  1035.6 47.1 %copy-start.29 = (f32[1,1,2,32]{3,2,1,0:T(2,128)S(1)}, f32[1,1,2,32]{3,2,1,0:T(2,128)}, u32[]{:S(2)}) copy-start(f32[1,1,2,32]{3,2,1,0:T(2,128)} %get-tuple-element.136) | copy-start | bytes 772
  1036.8 47.7 %copy-start.16 = (f32[2,32]{1,0:T(2,128)S(1)}, f32[2,32]{1,0:T(2,128)}, u32[]{:S(2)}) copy-start(f32[2,32]{1,0:T(2,128)} %copy-done.15) | copy-start | bytes 772
  1036.9 47.2 %collective-permute-start.10 = (bf16[1,2,32,512]{3,2,1,0:T(8,128)(2,1)S(1)}, bf16[1,2,32,512]{3,2,1,0:T(8,128)(2,1)S(1)}, u32[]{:S(2)}, u32[]{:S(2)}) collective-permute-start(bf16[1,2,32,512]{3,2,1,0:T(8,128)(2,1)S(1)} %pad_maximum_fusion.13), channel_id=1, source_target_pairs={{8,0},{16,8},{24,16},{9,1},{17,9},{25,17},{10,2},{18,10},{26,18},{... | collective-permute-start | bytes 196616 | tf_op jit(solution)/shard_map/ppermute | solution.py:41
  1038.2 45.9 %collective-permute-start.9 = (bf16[1,2,32,512]{3,2,1,0:T(8,128)(2,1)S(1)}, bf16[1,2,32,512]{3,2,1,0:T(8,128)(2,1)S(1)}, u32[]{:S(2)}, u32[]{:S(2)}) collective-permute-start(bf16[1,2,32,512]{3,2,1,0:T(8,128)(2,1)S(1)} %pad_maximum_fusion.13), channel_id=1, source_target_pairs={{0,8},{8,16},{16,24},{1,9},{9,17},{17,25},{2,10},{10,18},{18,26},{... | collective-permute-start | bytes 196616 | tf_op jit(solution)/shard_map/ppermute | solution.py:39
  1085.1 1.2 copy-start.2
  1098.4 1.9 copy-start.11
  1098.6 1.8 copy-start.21
  1100.3 110.9 %copy-start.5 = (f32[1,2,32,256]{3,2,1,0:T(8,128)}, f32[1,2,32,256]{3,2,1,0:T(8,128)S(1)}, u32[]{:S(2)}) copy-start(f32[1,2,32,256]{3,2,1,0:T(8,128)S(1)} %get-tuple-element.37) | copy-start | bytes 196612
  1104.1 26.2 %collective-permute-start.12 = (bf16[1,2,32,1024]{3,2,1,0:T(8,128)(2,1)S(1)}, bf16[1,2,32,1024]{3,2,1,0:T(8,128)(2,1)S(1)}, u32[]{:S(2)}, u32[]{:S(2)}) collective-permute-start(bf16[1,2,32,1024]{3,2,1,0:T(8,128)(2,1)S(1)} %fusion.21), channel_id=1, source_target_pairs={{8,0},{16,8},{24,16},{9,1},{17,9},{25,17},{10,2},{18,10},{26,18},{... | collective-permute-start | bytes 393224 | tf_op jit(solution)/shard_map/ppermute | solution.py:41
  1105.4 24.9 %collective-permute-start.11 = (bf16[1,2,32,1024]{3,2,1,0:T(8,128)(2,1)S(1)}, bf16[1,2,32,1024]{3,2,1,0:T(8,128)(2,1)S(1)}, u32[]{:S(2)}, u32[]{:S(2)}) collective-permute-start(bf16[1,2,32,1024]{3,2,1,0:T(8,128)(2,1)S(1)} %fusion.21), channel_id=1, source_target_pairs={{0,8},{8,16},{16,24},{1,9},{9,17},{17,25},{2,10},{10,18},{18,26},{... | collective-permute-start | bytes 393224 | tf_op jit(solution)/shard_map/ppermute | solution.py:39
  1199.5 11.7 copy-start.22
  1199.5 12.4 copy-start.9
  1213.5 1.6 copy-start.4
  1248.6 11.5 copy-start.23
  1248.6 11.5 copy-start.24
  1248.6 944.5 %all-reduce.15.cloned.1.call-start = ((), (), s32[]{:S(2)}) async-start(), calls=%async_computation.2 | async-start | bytes 13107200 | tf_op jit(solution)/shard_map/psum | solution.py:240
  1250.7 9.5 collective-permute-start.14
  1252.0 8.2 collective-permute-start.13
  2070.4 12.9 copy-start.14
  2126.7 97.7 %copy-start.10 = (f32[2,1,1024]{2,1,0:T(1,128)S(1)}, f32[2,1,1024]{2,1,0:T(1,128)}, u32[]{:S(2)}) copy-start(f32[2,1,1024]{2,1,0:T(1,128)} %param.27) | copy-start | bytes 24580
  2126.7 97.7 %copy-start.19 = (f32[2,1,1024]{2,1,0:T(1,128)S(1)}, f32[2,1,1024]{2,1,0:T(1,128)}, u32[]{:S(2)}) copy-start(f32[2,1,1024]{2,1,0:T(1,128)} %param.29) | copy-start | bytes 24580
  2126.7 97.7 %copy-start.20 = (f32[2,1,1024]{2,1,0:T(1,128)S(1)}, f32[2,1,1024]{2,1,0:T(1,128)}, u32[]{:S(2)}) copy-start(f32[2,1,1024]{2,1,0:T(1,128)} %param.28) | copy-start | bytes 24580
  2126.7 98.4 %copy-start.18 = (f32[3,256]{1,0:T(4,128)S(1)}, f32[3,256]{1,0:T(4,128)}, u32[]{:S(2)}) copy-start(f32[3,256]{1,0:T(4,128)} %param.30) | copy-start | bytes 9220
  2126.7 98.4 %copy-start.25 = (f32[3,256]{1,0:T(4,128)S(1)}, f32[3,256]{1,0:T(4,128)}, u32[]{:S(2)}) copy-start(f32[3,256]{1,0:T(4,128)} %param.32) | copy-start | bytes 9220
  2126.7 98.4 %copy-start.26 = (f32[3,256]{1,0:T(4,128)S(1)}, f32[3,256]{1,0:T(4,128)}, u32[]{:S(2)}) copy-start(f32[3,256]{1,0:T(4,128)} %param.31) | copy-start | bytes 9220
Sparse Core Ops, SparseCore 0:
  21.4 1004.2 all-gather.2
  1248.7 817.5 reduce-scatter.1
  2068.7 124.3 all-reduce.14
